TPU v7x, 256 devices: a whole 4x4x8 slice. The times are simulated.
256 devices in a mesh: src: 16 (over z, y_hi), tgt: 16 (over x, y_lo, core).
Axes of the slice: x: 4, y: 4 (y_hi: 2, y_lo: 2; y = y_hi * 2 + y_lo), z: 8, core: 2. Of those that a mesh axis runs over, the one named last changes fastest.
Arguments:
- frame_one: bfloat16 [256, 256, 128], P(('src', 'tgt')), may hold values from -36 to 36
- frame_two: bfloat16 [256, 256, 128], P(('src', 'tgt')), may hold values from -36 to 36
- conv_weight: bfloat16 [9, 128, 128], replicated, may hold values from -0.1875 to 0.1875
- proj_weight: bfloat16 [128, 128], replicated, may hold values from -0.5 to 0.5
Outputs:
- flow_forward: float32 [2, 256, 256], P(None, ('src', 'tgt'))
- flow_backward: float32 [2, 256, 256], P(None, ('src', 'tgt'))
All inputs are finite; a program needn't handle non-finite values.
Results may differ from a plain program's by a relative error of at most 0.012.
The roundings to bfloat16 on the way count: a program that leaves them out, or rounds other values in their place, can miss the bound.
Values may be sent and summed in bfloat16 or wider, within the bound.
A program may use at most 64 MiB of HBM per device.

v0:
```python
import math
import jax
import jax.numpy as jnp
from jax import lax
from jax.sharding import PartitionSpec as P


def padded_2(block, sides, width):
    for axis, dim in sides:
        count = lax.axis_size(axis)
        forward = [(i, i + 1) for i in range(count - 1)]
        backward = [(target, source) for source, target in forward]
        low = lax.ppermute(
            lax.slice_in_dim(block, block.shape[dim] - width, None, axis=dim), axis, forward
        )
        high = lax.ppermute(lax.slice_in_dim(block, 0, width, axis=dim), axis, backward)
        block = jnp.concatenate([low, block, high], axis=dim)
    return block


def merged(value, axis, join):
    pieces = jax.tree.map(lambda part: lax.all_gather(part, axis), value)
    head = jax.tree.map(lambda part: part[0], pieces)
    tail = jax.tree.map(lambda part: part[1:], pieces)
    subtotal, _ = lax.scan(lambda subtotal, piece: (join(subtotal, piece), None), head, tail)
    return subtotal


def encode(stacked, conv_weight, proj_weight):
    padded = padded_2(stacked, ((("src", "tgt"), 1),), 1)
    padded = jnp.pad(padded, ((0, 0), (0, 0), (1, 1), (0, 0)))
    strip_rows, columns = (stacked.shape[1], stacked.shape[2])
    total = jnp.zeros(stacked.shape, jnp.float32)
    for offset_row in range(3):
        for offset_col in range(3):
            window = padded[
                :, offset_row : offset_row + strip_rows, offset_col : offset_col + columns, :
            ]
            total = total + jnp.dot(
                window, conv_weight[3 * offset_row + offset_col], preferred_element_type=jnp.float32
            )
    hidden = jax.nn.relu(total).astype(jnp.bfloat16)
    mixed = stacked.astype(jnp.float32) + jnp.dot(
        hidden, proj_weight, preferred_element_type=jnp.float32
    )
    return mixed.astype(jnp.bfloat16)


def merge_pair(former, latter):
    highest = jnp.maximum(former[0], latter[0])
    keep_former = jnp.exp(former[0] - highest)
    keep_latter = jnp.exp(latter[0] - highest)
    return (
        highest,
        former[1] * keep_former + latter[1] * keep_latter,
        former[2] * keep_former + latter[2] * keep_latter,
        former[3] * keep_former + latter[3] * keep_latter,
    )


def tile_stats(piece_block, block_x, block_y, fixed_flat, fixed_x, fixed_y, factor):
    scores = (
        lax.dot_general(
            piece_block, fixed_flat, (((1,), (1,)), ((), ())), preferred_element_type=jnp.float32
        )
        * factor
    )
    row_top = jnp.max(scores, axis=1)
    row_weights = jnp.exp(scores - row_top[:, None])
    row_stats = (
        row_top,
        jnp.sum(row_weights, axis=1),
        jnp.sum(row_weights * fixed_x[None, :], axis=1),
        jnp.sum(row_weights * fixed_y[None, :], axis=1),
    )
    column_top = jnp.max(scores, axis=0)
    column_weights = jnp.exp(scores - column_top[None, :])
    column_stats = (
        column_top,
        jnp.sum(column_weights, axis=0),
        jnp.sum(column_weights * block_x[:, None], axis=0),
        jnp.sum(column_weights * block_y[:, None], axis=0),
    )
    return (row_stats, column_stats)


def on_device(frame_one, frame_two, conv_weight, proj_weight):
    features = encode(jnp.stack([frame_one, frame_two]), conv_weight, proj_weight)
    source_feat = features[0]
    target_feat = features[1]
    strip_rows, columns, channels = frame_one.shape
    src_index = lax.axis_index("src")
    tgt_index = lax.axis_index("tgt")
    src_count = lax.axis_size("src")
    tgt_count = lax.axis_size("tgt")
    factor = 1.0 / math.sqrt(channels)
    source_pixels = strip_rows * tgt_count * columns
    target_pixels = strip_rows * src_count * columns
    own_pixels = strip_rows * columns

    def pixel_coords(row_numbers):
        coord_y = jnp.repeat(row_numbers.astype(jnp.float32), columns)
        coord_x = jnp.tile(jnp.arange(columns, dtype=jnp.float32), row_numbers.shape[0])
        return (coord_x, coord_y)

    def empty_stats(count):
        zeros_line = jnp.zeros((count,), jnp.float32)
        return (jnp.full((count,), -jnp.inf, jnp.float32), zeros_line, zeros_line, zeros_line)

    target_tile = lax.all_gather(target_feat, "src", axis=0, tiled=True)
    whole_row = jnp.arange(strip_rows * src_count, dtype=jnp.int32)
    tile_x, tile_y = pixel_coords(
        (whole_row // strip_rows * tgt_count + tgt_index) * strip_rows + whole_row % strip_rows
    )
    fixed_flat = target_tile.reshape(-1, channels)
    shard_piece = lax.all_gather(source_feat, "tgt", axis=0, tiled=True)
    piece_rows = shard_piece.shape[0]
    block_rows = math.gcd(piece_rows, max(1, 512 // columns))
    blocks = piece_rows // block_rows
    block_size = block_rows * columns
    piece_x, piece_y = pixel_coords(
        src_index * tgt_count * strip_rows + jnp.arange(piece_rows, dtype=jnp.int32)
    )

    def block_step(fixed_acc, block_item):
        piece_block, block_x, block_y = block_item
        row_stats, column_stats = tile_stats(
            piece_block, block_x, block_y, fixed_flat, tile_x, tile_y, factor
        )
        return (merge_pair(fixed_acc, column_stats), row_stats)

    fixed_acc, row_parts = lax.scan(
        block_step,
        (empty_stats(target_pixels), empty_stats(source_pixels))[0],
        (
            shard_piece.reshape(blocks, block_size, channels),
            piece_x.reshape(blocks, block_size),
            piece_y.reshape(blocks, block_size),
        ),
    )
    placed = tuple((segment.reshape(-1) for segment in row_parts))
    fixed_acc, piece_acc = (fixed_acc, placed)
    source_stats, target_stats = (piece_acc, fixed_acc)
    own_x, own_y = pixel_coords(
        (src_index * tgt_count + tgt_index) * strip_rows + jnp.arange(strip_rows, dtype=jnp.int32)
    )
    merged_rows = merged(source_stats, "tgt", merge_pair)
    merged_cols = merged(target_stats, "src", merge_pair)
    source_sums = [
        lax.dynamic_slice_in_dim(member, tgt_index * own_pixels, own_pixels, 0)
        for member in merged_rows[1:]
    ]
    target_sums = [
        lax.dynamic_slice_in_dim(member, src_index * own_pixels, own_pixels, 0)
        for member in merged_cols[1:]
    ]
    flow_forward = jnp.stack(
        [source_sums[1] / source_sums[0] - own_x, source_sums[2] / source_sums[0] - own_y]
    ).reshape(2, strip_rows, columns)
    flow_backward = jnp.stack(
        [target_sums[1] / target_sums[0] - own_x, target_sums[2] / target_sums[0] - own_y]
    ).reshape(2, strip_rows, columns)
    return (flow_forward, flow_backward)


def solution(mesh):
    in_specs = (P(("src", "tgt"), None, None), P(("src", "tgt"), None, None), P(), P())
    out_specs = (P(None, ("src", "tgt"), None), P(None, ("src", "tgt"), None))
    return jax.shard_map(
        on_device, mesh=mesh, in_specs=in_specs, out_specs=out_specs, check_vma=False
    )
```

profile of v0, /device:TPU:16, one launch (start us, length us, event | category | flops | bytes accessed | tf_op | source)
XLA Modules:
  0.0 487.1 jit_solution(11007126470495487609)
XLA Ops:
  8.1 1.9 collective-permute-start
  10.0 5.8 %collective-permute-start.1 = (bf16[2,1,256,128]{3,2,1,0:T(8,128)(2,1)S(1)}, bf16[2,1,256,128]{3,2,1,0:T(8,128)(2,1)S(1)}, u32[]{:S(2)}, u32[]{:S(2)}) collective-permute-start(bf16[2,1,256,128]{3,2,1,0:T(8,128)(2,1)S(1)} %pad_maximum_fusion), channel_id=1, source_target_pairs={{1,0},{2,1},{3,2},{4,3},{5,4},{6,5},{7,6},{8,7},{9,8},{10,9},{11,1... | collective-permute-start | bytes 393224 | tf_op jit(solution)/shard_map/ppermute | solution.py:16
  16.5 1.8 collective-permute-done.1
  29.7 39.2 %all-gather.11.cloned.1.call-done = bf16[16,256,128]{2,1,0:T(8,128)(2,1)} async-done(((bf16[1,256,128]{2,1,0:T(8,128)(2,1)}), bf16[16,256,128]{2,1,0:T(8,128)(2,1)}) %all-gather.11.cloned.1.call-update) | async-done | bytes 1048592 | tf_op jit(solution)/shard_map/all_gather | solution.py:116
  69.0 79.3 %all-gather.13.cloned.1.call-done = bf16[16,256,128]{2,1,0:T(8,128)(2,1)} async-done(((bf16[1,256,128]{2,1,0:T(8,128)(2,1)}), bf16[16,256,128]{2,1,0:T(8,128)(2,1)}) %all-gather.13.cloned.1.call-update) | async-done | bytes 1048592 | tf_op jit(solution)/shard_map/all_gather | solution.py:110
  148.3 94.9 %while.59 = (s32[]{:T(128)}, f32[4096]{0:T(1024)S(1)}, f32[4096]{0:T(1024)S(1)}, f32[4096]{0:T(1024)S(1)}, f32[4096]{0:T(1024)S(1)}, /*index=5*/f32[8,512]{1,0:T...) while((s32[]{:T(128)}, f32[4096]{0:T(1024)S(1)}, ...), condition=%wide.region_9.10_spmd.clone, body=%wide.region_0.9_spmd.clone.sunk | while | flops 570484736 | bytes 18488048 | solution.py:132
  148.3 2.6 multiply_reduce_fusion.8
  151.1 8.7 %multiply_reduce_fusion.9 = (f32[512]{0:T(512)S(1)}, f32[512]{0:T(512)S(1)}, f32[512]{0:T(512)S(1)}, f32[4096]{0:T(1024)S(1)}, f32[4096]{0:T(1024)S(1)}, /*index=5*/f32[4096]{0:T(1024)S(1)}) fusion(f32[512,4096]{1,0:T(8,128)S(1)} %get-tuple-element.596, f32[4096]{0:T(1024)S(1)} %bitcast.168, f32[512]{0:T(512)S(1)} %get-tuple-element.597, ...), kind=kLoop, calls=%fused_computation.20.clone.1 | loop fusion | flops 27249152 | bytes 8499200 | tf_op jit(solution)/shard_map/while/body/eval_jaxpr/reduce_sum | solution.py:74
  160.2 2.6 multiply_reduce_fusion.8
  162.9 8.7 %multiply_reduce_fusion.9 = (f32[512]{0:T(512)S(1)}, f32[512]{0:T(512)S(1)}, f32[512]{0:T(512)S(1)}, f32[4096]{0:T(1024)S(1)}, f32[4096]{0:T(1024)S(1)}, /*index=5*/f32[4096]{0:T(1024)S(1)}) fusion(f32[512,4096]{1,0:T(8,128)S(1)} %get-tuple-element.596, f32[4096]{0:T(1024)S(1)} %bitcast.168, f32[512]{0:T(512)S(1)} %get-tuple-element.597, ...), kind=kLoop, calls=%fused_computation.20.clone.1 | loop fusion | flops 27249152 | bytes 8499200 | tf_op jit(solution)/shard_map/while/body/eval_jaxpr/reduce_sum | solution.py:74
  172.0 2.6 multiply_reduce_fusion.8
  174.8 8.7 %multiply_reduce_fusion.9 = (f32[512]{0:T(512)S(1)}, f32[512]{0:T(512)S(1)}, f32[512]{0:T(512)S(1)}, f32[4096]{0:T(1024)S(1)}, f32[4096]{0:T(1024)S(1)}, /*index=5*/f32[4096]{0:T(1024)S(1)}) fusion(f32[512,4096]{1,0:T(8,128)S(1)} %get-tuple-element.596, f32[4096]{0:T(1024)S(1)} %bitcast.168, f32[512]{0:T(512)S(1)} %get-tuple-element.597, ...), kind=kLoop, calls=%fused_computation.20.clone.1 | loop fusion | flops 27249152 | bytes 8499200 | tf_op jit(solution)/shard_map/while/body/eval_jaxpr/reduce_sum | solution.py:74
  183.9 2.6 multiply_reduce_fusion.8
  186.7 8.7 %multiply_reduce_fusion.9 = (f32[512]{0:T(512)S(1)}, f32[512]{0:T(512)S(1)}, f32[512]{0:T(512)S(1)}, f32[4096]{0:T(1024)S(1)}, f32[4096]{0:T(1024)S(1)}, /*index=5*/f32[4096]{0:T(1024)S(1)}) fusion(f32[512,4096]{1,0:T(8,128)S(1)} %get-tuple-element.596, f32[4096]{0:T(1024)S(1)} %bitcast.168, f32[512]{0:T(512)S(1)} %get-tuple-element.597, ...), kind=kLoop, calls=%fused_computation.20.clone.1 | loop fusion | flops 27249152 | bytes 8499200 | tf_op jit(solution)/shard_map/while/body/eval_jaxpr/reduce_sum | solution.py:74
  195.7 2.6 multiply_reduce_fusion.8
  198.5 8.7 %multiply_reduce_fusion.9 = (f32[512]{0:T(512)S(1)}, f32[512]{0:T(512)S(1)}, f32[512]{0:T(512)S(1)}, f32[4096]{0:T(1024)S(1)}, f32[4096]{0:T(1024)S(1)}, /*index=5*/f32[4096]{0:T(1024)S(1)}) fusion(f32[512,4096]{1,0:T(8,128)S(1)} %get-tuple-element.596, f32[4096]{0:T(1024)S(1)} %bitcast.168, f32[512]{0:T(512)S(1)} %get-tuple-element.597, ...), kind=kLoop, calls=%fused_computation.20.clone.1 | loop fusion | flops 27249152 | bytes 8499200 | tf_op jit(solution)/shard_map/while/body/eval_jaxpr/reduce_sum | solution.py:74
  207.6 2.6 multiply_reduce_fusion.8
  210.4 8.7 %multiply_reduce_fusion.9 = (f32[512]{0:T(512)S(1)}, f32[512]{0:T(512)S(1)}, f32[512]{0:T(512)S(1)}, f32[4096]{0:T(1024)S(1)}, f32[4096]{0:T(1024)S(1)}, /*index=5*/f32[4096]{0:T(1024)S(1)}) fusion(f32[512,4096]{1,0:T(8,128)S(1)} %get-tuple-element.596, f32[4096]{0:T(1024)S(1)} %bitcast.168, f32[512]{0:T(512)S(1)} %get-tuple-element.597, ...), kind=kLoop, calls=%fused_computation.20.clone.1 | loop fusion | flops 27249152 | bytes 8499200 | tf_op jit(solution)/shard_map/while/body/eval_jaxpr/reduce_sum | solution.py:74
  219.5 2.6 multiply_reduce_fusion.8
  222.3 8.7 %multiply_reduce_fusion.9 = (f32[512]{0:T(512)S(1)}, f32[512]{0:T(512)S(1)}, f32[512]{0:T(512)S(1)}, f32[4096]{0:T(1024)S(1)}, f32[4096]{0:T(1024)S(1)}, /*index=5*/f32[4096]{0:T(1024)S(1)}) fusion(f32[512,4096]{1,0:T(8,128)S(1)} %get-tuple-element.596, f32[4096]{0:T(1024)S(1)} %bitcast.168, f32[512]{0:T(512)S(1)} %get-tuple-element.597, ...), kind=kLoop, calls=%fused_computation.20.clone.1 | loop fusion | flops 27249152 | bytes 8499200 | tf_op jit(solution)/shard_map/while/body/eval_jaxpr/reduce_sum | solution.py:74
  231.3 2.6 multiply_reduce_fusion.8
  234.1 8.7 %multiply_reduce_fusion.9 = (f32[512]{0:T(512)S(1)}, f32[512]{0:T(512)S(1)}, f32[512]{0:T(512)S(1)}, f32[4096]{0:T(1024)S(1)}, f32[4096]{0:T(1024)S(1)}, /*index=5*/f32[4096]{0:T(1024)S(1)}) fusion(f32[512,4096]{1,0:T(8,128)S(1)} %get-tuple-element.596, f32[4096]{0:T(1024)S(1)} %bitcast.168, f32[512]{0:T(512)S(1)} %get-tuple-element.597, ...), kind=kLoop, calls=%fused_computation.20.clone.1 | loop fusion | flops 27249152 | bytes 8499200 | tf_op jit(solution)/shard_map/while/body/eval_jaxpr/reduce_sum | solution.py:74
  243.2 20.8 %all-gather.4 = f32[16,1,4096]{2,1,0:T(1,128)S(1)} all-gather(f32[1,1,4096]{2,1,0:T(1,128)S(1)} %reshape.124), channel_id=1, replica_groups=mesh['src'=16,'tgt'=16] {'tgt'}, dimensions={0}, use_global_device_ids=true | all-gather | bytes 278528 | tf_op jit(solution)/shard_map/all_gather | solution.py:22
  264.1 17.0 %all-gather.5 = f32[16,1,4096]{2,1,0:T(1,128)S(1)} all-gather(f32[1,1,4096]{2,1,0:T(1,128)S(1)} %reshape.126), channel_id=1, replica_groups=mesh['src'=16,'tgt'=16] {'tgt'}, dimensions={0}, use_global_device_ids=true | all-gather | bytes 278528 | tf_op jit(solution)/shard_map/all_gather | solution.py:22
  281.2 18.5 %all-gather.6 = f32[16,1,4096]{2,1,0:T(1,128)S(1)} all-gather(f32[1,1,4096]{2,1,0:T(1,128)S(1)} %reshape.128), channel_id=1, replica_groups=mesh['src'=16,'tgt'=16] {'tgt'}, dimensions={0}, use_global_device_ids=true | all-gather | bytes 278528 | tf_op jit(solution)/shard_map/all_gather | solution.py:22
  299.7 17.0 %all-gather.7 = f32[16,1,4096]{2,1,0:T(1,128)S(1)} all-gather(f32[1,1,4096]{2,1,0:T(1,128)S(1)} %reshape.130), channel_id=1, replica_groups=mesh['src'=16,'tgt'=16] {'tgt'}, dimensions={0}, use_global_device_ids=true | all-gather | bytes 278528 | tf_op jit(solution)/shard_map/all_gather | solution.py:22
  316.7 38.6 %all-gather = f32[65536]{0:T(1024)S(1)} all-gather(f32[4096]{0:T(1024)S(1)} %get-tuple-element.191), channel_id=2, replica_groups=mesh['src'=16,'tgt'=16] {'src'}, dimensions={0}, use_global_device_ids=true | all-gather | bytes 278528 | tf_op jit(solution)/shard_map/all_gather | solution.py:22
  355.3 40.5 %all-gather.1 = f32[65536]{0:T(1024)S(1)} all-gather(f32[4096]{0:T(1024)S(1)} %get-tuple-element.192), channel_id=3, replica_groups=mesh['src'=16,'tgt'=16] {'src'}, dimensions={0}, use_global_device_ids=true | all-gather | bytes 278528 | tf_op jit(solution)/shard_map/all_gather | solution.py:22
  395.9 37.1 %all-gather.2 = f32[65536]{0:T(1024)S(1)} all-gather(f32[4096]{0:T(1024)S(1)} %get-tuple-element.193), channel_id=4, replica_groups=mesh['src'=16,'tgt'=16] {'src'}, dimensions={0}, use_global_device_ids=true | all-gather | bytes 278528 | tf_op jit(solution)/shard_map/all_gather | solution.py:22
  433.0 40.5 %all-gather.3 = f32[65536]{0:T(1024)S(1)} all-gather(f32[4096]{0:T(1024)S(1)} %get-tuple-element.194), channel_id=5, replica_groups=mesh['src'=16,'tgt'=16] {'src'}, dimensions={0}, use_global_device_ids=true | all-gather | bytes 278528 | tf_op jit(solution)/shard_map/all_gather | solution.py:22
  474.1 2.4 while.57
  476.7 2.4 while.58
  (312 shorter events, 21.5 us)
Async XLA Ops:
  7.2 19.7 %copy-start = (bf16[128,128]{1,0:T(8,128)(2,1)S(1)}, bf16[128,128]{1,0:T(8,128)(2,1)}, u32[]{:S(2)}) copy-start(bf16[128,128]{1,0:T(8,128)(2,1)} %param.13) | copy-start | bytes 98308
  7.2 61.8 %all-gather.11.cloned.1.call-start = ((), (), s32[]{:S(2)}) async-start(), calls=%async_computation | async-start | bytes 1114112 | tf_op jit(solution)/shard_map/all_gather | solution.py:116
  8.1 8.4 %collective-permute-start = (bf16[2,1,256,128]{3,2,1,0:T(8,128)(2,1)S(1)}, bf16[2,1,256,128]{3,2,1,0:T(8,128)(2,1)S(1)}, u32[]{:S(2)}, u32[]{:S(2)}) collective-permute-start(bf16[2,1,256,128]{3,2,1,0:T(8,128)(2,1)S(1)} %pad_maximum_fusion), channel_id=1, source_target_pairs={{0,1},{1,2},{2,3},{3,4},{4,5},{5,6},{6,7},{7,8},{8,9},{9,10},{10,1... | collective-permute-start | bytes 393224 | tf_op jit(solution)/shard_map/ppermute | solution.py:13
  10.0 8.3 %collective-permute-start.1 = (bf16[2,1,256,128]{3,2,1,0:T(8,128)(2,1)S(1)}, bf16[2,1,256,128]{3,2,1,0:T(8,128)(2,1)S(1)}, u32[]{:S(2)}, u32[]{:S(2)}) collective-permute-start(bf16[2,1,256,128]{3,2,1,0:T(8,128)(2,1)S(1)} %pad_maximum_fusion), channel_id=1, source_target_pairs={{1,0},{2,1},{3,2},{4,3},{5,4},{6,5},{7,6},{8,7},{9,8},{10,9},{11,1... | collective-permute-start | bytes 393224 | tf_op jit(solution)/shard_map/ppermute | solution.py:16
  28.8 119.4 %all-gather.13.cloned.1.call-start = ((), (), s32[]{:S(2)}) async-start(), calls=%async_computation.1 | async-start | bytes 1114112 | tf_op jit(solution)/shard_map/all_gather | solution.py:110
Sparse Core Ops, SparseCore 0:
  28.9 39.9 all-gather.10
  71.5 76.6 all-gather.12
where the time goes:
time: 488 us; the launch traced here: 487 us
  blocking collectives  230 us (47%)
  waiting for transfers between devices  122 us (25%)
  other arithmetic  73.2 us (15%)
  matrix products  29.9 us (6%)
  between operations  14.4 us (3%)
  local copies, waits for them, and re-layouts  7.8 us (2%)
  starting transfers between devices  7.75 us (2%)
    all_gather x8, blocking collectives, merged(): pieces = jax.tree.map(lambda part: lax.all_gather(part, axis), value)  230 us
    all_gather x1, waiting for transfers between devices, on_device(): target_tile = lax.all_gather(target_feat, 'src', axis=0, tiled=True)  79.3 us
    reduce_sum x8, other arithmetic, tile_stats(): jnp.sum(row_weights * fixed_y[None, :], axis=1)  69.7 us
    all_gather x1, waiting for transfers between devices, on_device(): shard_piece = lax.all_gather(source_feat, 'tgt', axis=0, tiled=True)  39.2 us
    dot_general x8, matrix products, tile_stats(): lax.dot_general(piece_block, fixed_flat, (((1,), (1,)), ((), ())), prefer...  21.2 us
  transfers between devices with their start and end apart: 4, of which 4 were waited for; matrix products, arithmetic and copies ran while one was open for 0% of the time, Pallas kernels for 0%

commit v1 on v0

--- a/solution.py
+++ b/solution.py
@@ -113,7 +113,9 @@
         (whole_row // strip_rows * tgt_count + tgt_index) * strip_rows + whole_row % strip_rows
     )
     fixed_flat = target_tile.reshape(-1, channels)
-    shard_piece = lax.all_gather(source_feat, "tgt", axis=0, tiled=True)
+    shard_piece = jnp.concatenate(
+        lax.all_to_all(jnp.stack([source_feat] * lax.axis_size("tgt")), "tgt", 0, 0), axis=0
+    )
     piece_rows = shard_piece.shape[0]
     block_rows = math.gcd(piece_rows, max(1, 512 // columns))
     blocks = piece_rows // block_rows

time: 488 us -> 453 us (0.928)
  waiting for transfers between devices: 122 us -> 77.4 us
  starting transfers between devices: 7.75 us -> 16 us
    all_gather x1 -> x0, waiting for transfers between devices: 39.2 us -> none  [on_device(): shard_piece = lax.all_gather(source_feat, 'tgt', axis=0, tiled=True)]
    all_gather x1, waiting for transfers between devices: 79.3 us -> 58.6 us  [on_device(): target_tile = lax.all_gather(target_feat, 'src', axis=0, tiled=True)]
    all_to_all x0 -> x1, waiting for transfers between devices: none -> 16.3 us  [on_device(): lax.all_to_all(jnp.stack([source_feat] * lax.axis_size('tgt')), 'tgt', 0, 0)]
    all_to_all x0 -> x1, starting transfers between devices: none -> 8.3 us  [on_device(): lax.all_to_all(jnp.stack([source_feat] * lax.axis_size('tgt')), 'tgt', 0, 0)]
where the time goes in v1:
time: 453 us; the launch traced here: 452 us
  blocking collectives  230 us (51%)
  waiting for transfers between devices  77.4 us (17%)
  other arithmetic  73.2 us (16%)
  matrix products  29.3 us (6%)
  starting transfers between devices  16 us (4%)
  between operations  14.4 us (3%)
  local copies, waits for them, and re-layouts  9 us (2%)
    all_gather x8, blocking collectives, merged(): pieces = jax.tree.map(lambda part: lax.all_gather(part, axis), value)  230 us
    reduce_sum x8, other arithmetic, tile_stats(): jnp.sum(row_weights * fixed_y[None, :], axis=1)  69.7 us
    all_gather x1, waiting for transfers between devices, on_device(): target_tile = lax.all_gather(target_feat, 'src', axis=0, tiled=True)  58.6 us
    dot_general x8, matrix products, tile_stats(): lax.dot_general(piece_block, fixed_flat, (((1,), (1,)), ((), ())), prefer...  20.6 us
    all_to_all x1, waiting for transfers between devices, on_device(): lax.all_to_all(jnp.stack([source_feat] * lax.axis_size('tgt')), 'tgt', 0, 0)  16.3 us
  transfers between devices with their start and end apart: 4, of which 4 were waited for; matrix products, arithmetic and copies ran while one was open for 0% of the time, Pallas kernels for 0%

profile of v1, /device:TPU:16, one launch (start us, length us, event | category | flops | bytes accessed | tf_op | source)
XLA Modules:
  0.0 451.6 jit_solution(11867758196710336091)
XLA Ops:
  8.1 1.9 collective-permute-start
  10.0 5.8 %collective-permute-start.1 = (bf16[2,1,256,128]{3,2,1,0:T(8,128)(2,1)S(1)}, bf16[2,1,256,128]{3,2,1,0:T(8,128)(2,1)S(1)}, u32[]{:S(2)}, u32[]{:S(2)}) collective-permute-start(bf16[2,1,256,128]{3,2,1,0:T(8,128)(2,1)S(1)} %pad_maximum_fusion), channel_id=1, source_target_pairs={{1,0},{2,1},{3,2},{4,3},{5,4},{6,5},{7,6},{8,7},{9,8},{10,9},{11,1... | collective-permute-start | bytes 393224 | tf_op jit(solution)/shard_map/ppermute | solution.py:16
  30.0 8.3 %all-to-all-start = ((bf16[16,1,256,128]{3,2,1,0:T(8,128)(2,1)}), bf16[16,1,256,128]{3,2,1,0:T(8,128)(2,1)S(1)}, u32[]{:S(2)}, u32[]{:S(2)}) async-start(bf16[16,1,256,128]{3,2,1,0:T(8,128)(2,1)} %stack.36), calls=%async_computation | async-start | bytes 2097152 | tf_op jit(solution)/shard_map/all_to_all | solution.py:117
  38.5 16.3 %all-to-all-done = bf16[16,1,256,128]{3,2,1,0:T(8,128)(2,1)S(1)} async-done(((bf16[16,1,256,128]{3,2,1,0:T(8,128)(2,1)}), bf16[16,1,256,128]{3,2,1,0:T(8,128)(2,1)S(1)}, u32[]{:S(2)}, u32[]{:S(2)}) %all-to-all-start) | async-done | bytes 1048608 | tf_op jit(solution)/shard_map/all_to_all | solution.py:117
  54.8 58.6 %all-gather.10.cloned.1.call-done = bf16[16,256,128]{2,1,0:T(8,128)(2,1)} async-done(((bf16[1,256,128]{2,1,0:T(8,128)(2,1)}), bf16[16,256,128]{2,1,0:T(8,128)(2,1)}) %all-gather.10.cloned.1.call-update) | async-done | bytes 1048592 | tf_op jit(solution)/shard_map/all_gather | solution.py:110
  113.4 94.3 %while.59 = (s32[]{:T(128)}, f32[4096]{0:T(1024)S(1)}, f32[4096]{0:T(1024)S(1)}, f32[4096]{0:T(1024)S(1)}, f32[4096]{0:T(1024)S(1)}, /*index=5*/f32[8,512]{1,0:T...) while((s32[]{:T(128)}, f32[4096]{0:T(1024)S(1)}, ...), condition=%wide.region_9.10_spmd.clone, body=%wide.region_0.9_spmd.clone.sunk | while | flops 570484736 | bytes 18487540 | solution.py:134
  113.4 2.6 multiply_reduce_fusion.8
  116.1 8.7 %multiply_reduce_fusion.9 = (f32[512]{0:T(512)S(1)}, f32[512]{0:T(512)S(1)}, f32[512]{0:T(512)S(1)}, f32[4096]{0:T(1024)S(1)}, f32[4096]{0:T(1024)S(1)}, /*index=5*/f32[4096]{0:T(1024)S(1)}) fusion(f32[512,4096]{1,0:T(8,128)S(1)} %get-tuple-element.596, f32[4096]{0:T(1024)S(1)} %bitcast.171, f32[512]{0:T(512)S(1)} %get-tuple-element.597, ...), kind=kLoop, calls=%fused_computation.20.clone.1 | loop fusion | flops 27249152 | bytes 8499200 | tf_op jit(solution)/shard_map/while/body/eval_jaxpr/reduce_sum | solution.py:74
  125.2 2.6 multiply_reduce_fusion.8
  127.9 8.7 %multiply_reduce_fusion.9 = (f32[512]{0:T(512)S(1)}, f32[512]{0:T(512)S(1)}, f32[512]{0:T(512)S(1)}, f32[4096]{0:T(1024)S(1)}, f32[4096]{0:T(1024)S(1)}, /*index=5*/f32[4096]{0:T(1024)S(1)}) fusion(f32[512,4096]{1,0:T(8,128)S(1)} %get-tuple-element.596, f32[4096]{0:T(1024)S(1)} %bitcast.171, f32[512]{0:T(512)S(1)} %get-tuple-element.597, ...), kind=kLoop, calls=%fused_computation.20.clone.1 | loop fusion | flops 27249152 | bytes 8499200 | tf_op jit(solution)/shard_map/while/body/eval_jaxpr/reduce_sum | solution.py:74
  137.0 2.6 multiply_reduce_fusion.8
  139.7 8.7 %multiply_reduce_fusion.9 = (f32[512]{0:T(512)S(1)}, f32[512]{0:T(512)S(1)}, f32[512]{0:T(512)S(1)}, f32[4096]{0:T(1024)S(1)}, f32[4096]{0:T(1024)S(1)}, /*index=5*/f32[4096]{0:T(1024)S(1)}) fusion(f32[512,4096]{1,0:T(8,128)S(1)} %get-tuple-element.596, f32[4096]{0:T(1024)S(1)} %bitcast.171, f32[512]{0:T(512)S(1)} %get-tuple-element.597, ...), kind=kLoop, calls=%fused_computation.20.clone.1 | loop fusion | flops 27249152 | bytes 8499200 | tf_op jit(solution)/shard_map/while/body/eval_jaxpr/reduce_sum | solution.py:74
  148.8 2.6 multiply_reduce_fusion.8
  151.5 8.7 %multiply_reduce_fusion.9 = (f32[512]{0:T(512)S(1)}, f32[512]{0:T(512)S(1)}, f32[512]{0:T(512)S(1)}, f32[4096]{0:T(1024)S(1)}, f32[4096]{0:T(1024)S(1)}, /*index=5*/f32[4096]{0:T(1024)S(1)}) fusion(f32[512,4096]{1,0:T(8,128)S(1)} %get-tuple-element.596, f32[4096]{0:T(1024)S(1)} %bitcast.171, f32[512]{0:T(512)S(1)} %get-tuple-element.597, ...), kind=kLoop, calls=%fused_computation.20.clone.1 | loop fusion | flops 27249152 | bytes 8499200 | tf_op jit(solution)/shard_map/while/body/eval_jaxpr/reduce_sum | solution.py:74
  160.6 2.6 multiply_reduce_fusion.8
  163.3 8.7 %multiply_reduce_fusion.9 = (f32[512]{0:T(512)S(1)}, f32[512]{0:T(512)S(1)}, f32[512]{0:T(512)S(1)}, f32[4096]{0:T(1024)S(1)}, f32[4096]{0:T(1024)S(1)}, /*index=5*/f32[4096]{0:T(1024)S(1)}) fusion(f32[512,4096]{1,0:T(8,128)S(1)} %get-tuple-element.596, f32[4096]{0:T(1024)S(1)} %bitcast.171, f32[512]{0:T(512)S(1)} %get-tuple-element.597, ...), kind=kLoop, calls=%fused_computation.20.clone.1 | loop fusion | flops 27249152 | bytes 8499200 | tf_op jit(solution)/shard_map/while/body/eval_jaxpr/reduce_sum | solution.py:74
  172.4 2.6 multiply_reduce_fusion.8
  175.1 8.7 %multiply_reduce_fusion.9 = (f32[512]{0:T(512)S(1)}, f32[512]{0:T(512)S(1)}, f32[512]{0:T(512)S(1)}, f32[4096]{0:T(1024)S(1)}, f32[4096]{0:T(1024)S(1)}, /*index=5*/f32[4096]{0:T(1024)S(1)}) fusion(f32[512,4096]{1,0:T(8,128)S(1)} %get-tuple-element.596, f32[4096]{0:T(1024)S(1)} %bitcast.171, f32[512]{0:T(512)S(1)} %get-tuple-element.597, ...), kind=kLoop, calls=%fused_computation.20.clone.1 | loop fusion | flops 27249152 | bytes 8499200 | tf_op jit(solution)/shard_map/while/body/eval_jaxpr/reduce_sum | solution.py:74
  184.1 2.6 multiply_reduce_fusion.8
  186.8 8.7 %multiply_reduce_fusion.9 = (f32[512]{0:T(512)S(1)}, f32[512]{0:T(512)S(1)}, f32[512]{0:T(512)S(1)}, f32[4096]{0:T(1024)S(1)}, f32[4096]{0:T(1024)S(1)}, /*index=5*/f32[4096]{0:T(1024)S(1)}) fusion(f32[512,4096]{1,0:T(8,128)S(1)} %get-tuple-element.596, f32[4096]{0:T(1024)S(1)} %bitcast.171, f32[512]{0:T(512)S(1)} %get-tuple-element.597, ...), kind=kLoop, calls=%fused_computation.20.clone.1 | loop fusion | flops 27249152 | bytes 8499200 | tf_op jit(solution)/shard_map/while/body/eval_jaxpr/reduce_sum | solution.py:74
  195.9 2.6 multiply_reduce_fusion.8
  198.6 8.7 %multiply_reduce_fusion.9 = (f32[512]{0:T(512)S(1)}, f32[512]{0:T(512)S(1)}, f32[512]{0:T(512)S(1)}, f32[4096]{0:T(1024)S(1)}, f32[4096]{0:T(1024)S(1)}, /*index=5*/f32[4096]{0:T(1024)S(1)}) fusion(f32[512,4096]{1,0:T(8,128)S(1)} %get-tuple-element.596, f32[4096]{0:T(1024)S(1)} %bitcast.171, f32[512]{0:T(512)S(1)} %get-tuple-element.597, ...), kind=kLoop, calls=%fused_computation.20.clone.1 | loop fusion | flops 27249152 | bytes 8499200 | tf_op jit(solution)/shard_map/while/body/eval_jaxpr/reduce_sum | solution.py:74
  207.7 20.8 %all-gather.4 = f32[16,1,4096]{2,1,0:T(1,128)S(1)} all-gather(f32[1,1,4096]{2,1,0:T(1,128)S(1)} %reshape.122), channel_id=1, replica_groups=mesh['src'=16,'tgt'=16] {'tgt'}, dimensions={0}, use_global_device_ids=true | all-gather | bytes 278528 | tf_op jit(solution)/shard_map/all_gather | solution.py:22
  228.6 17.0 %all-gather.5 = f32[16,1,4096]{2,1,0:T(1,128)S(1)} all-gather(f32[1,1,4096]{2,1,0:T(1,128)S(1)} %reshape.124), channel_id=1, replica_groups=mesh['src'=16,'tgt'=16] {'tgt'}, dimensions={0}, use_global_device_ids=true | all-gather | bytes 278528 | tf_op jit(solution)/shard_map/all_gather | solution.py:22
  245.7 18.5 %all-gather.6 = f32[16,1,4096]{2,1,0:T(1,128)S(1)} all-gather(f32[1,1,4096]{2,1,0:T(1,128)S(1)} %reshape.126), channel_id=1, replica_groups=mesh['src'=16,'tgt'=16] {'tgt'}, dimensions={0}, use_global_device_ids=true | all-gather | bytes 278528 | tf_op jit(solution)/shard_map/all_gather | solution.py:22
  264.2 17.0 %all-gather.7 = f32[16,1,4096]{2,1,0:T(1,128)S(1)} all-gather(f32[1,1,4096]{2,1,0:T(1,128)S(1)} %reshape.128), channel_id=1, replica_groups=mesh['src'=16,'tgt'=16] {'tgt'}, dimensions={0}, use_global_device_ids=true | all-gather | bytes 278528 | tf_op jit(solution)/shard_map/all_gather | solution.py:22
  281.2 38.6 %all-gather = f32[65536]{0:T(1024)S(1)} all-gather(f32[4096]{0:T(1024)S(1)} %get-tuple-element.191), channel_id=2, replica_groups=mesh['src'=16,'tgt'=16] {'src'}, dimensions={0}, use_global_device_ids=true | all-gather | bytes 278528 | tf_op jit(solution)/shard_map/all_gather | solution.py:22
  319.8 40.4 %all-gather.1 = f32[65536]{0:T(1024)S(1)} all-gather(f32[4096]{0:T(1024)S(1)} %get-tuple-element.192), channel_id=3, replica_groups=mesh['src'=16,'tgt'=16] {'src'}, dimensions={0}, use_global_device_ids=true | all-gather | bytes 278528 | tf_op jit(solution)/shard_map/all_gather | solution.py:22
  360.3 37.1 %all-gather.2 = f32[65536]{0:T(1024)S(1)} all-gather(f32[4096]{0:T(1024)S(1)} %get-tuple-element.193), channel_id=4, replica_groups=mesh['src'=16,'tgt'=16] {'src'}, dimensions={0}, use_global_device_ids=true | all-gather | bytes 278528 | tf_op jit(solution)/shard_map/all_gather | solution.py:22
  397.4 40.5 %all-gather.3 = f32[65536]{0:T(1024)S(1)} all-gather(f32[4096]{0:T(1024)S(1)} %get-tuple-element.194), channel_id=5, replica_groups=mesh['src'=16,'tgt'=16] {'src'}, dimensions={0}, use_global_device_ids=true | all-gather | bytes 278528 | tf_op jit(solution)/shard_map/all_gather | solution.py:22
  438.6 2.4 while.57
  441.1 2.4 while.58
  (312 shorter events, 23.8 us)
Async XLA Ops:
  7.2 19.7 %copy-start = (bf16[128,128]{1,0:T(8,128)(2,1)S(1)}, bf16[128,128]{1,0:T(8,128)(2,1)}, u32[]{:S(2)}) copy-start(bf16[128,128]{1,0:T(8,128)(2,1)} %param.13) | copy-start | bytes 98308
  7.2 106.2 %all-gather.10.cloned.1.call-start = ((), (), s32[]{:S(2)}) async-start(), calls=%async_computation.1 | async-start | bytes 1114112 | tf_op jit(solution)/shard_map/all_gather | solution.py:110
  8.1 8.4 %collective-permute-start = (bf16[2,1,256,128]{3,2,1,0:T(8,128)(2,1)S(1)}, bf16[2,1,256,128]{3,2,1,0:T(8,128)(2,1)S(1)}, u32[]{:S(2)}, u32[]{:S(2)}) collective-permute-start(bf16[2,1,256,128]{3,2,1,0:T(8,128)(2,1)S(1)} %pad_maximum_fusion), channel_id=1, source_target_pairs={{0,1},{1,2},{2,3},{3,4},{4,5},{5,6},{6,7},{7,8},{8,9},{9,10},{10,1... | collective-permute-start | bytes 393224 | tf_op jit(solution)/shard_map/ppermute | solution.py:13
  10.0 8.3 %collective-permute-start.1 = (bf16[2,1,256,128]{3,2,1,0:T(8,128)(2,1)S(1)}, bf16[2,1,256,128]{3,2,1,0:T(8,128)(2,1)S(1)}, u32[]{:S(2)}, u32[]{:S(2)}) collective-permute-start(bf16[2,1,256,128]{3,2,1,0:T(8,128)(2,1)S(1)} %pad_maximum_fusion), channel_id=1, source_target_pairs={{1,0},{2,1},{3,2},{4,3},{5,4},{6,5},{7,6},{8,7},{9,8},{10,9},{11,1... | collective-permute-start | bytes 393224 | tf_op jit(solution)/shard_map/ppermute | solution.py:16
  30.0 24.8 %all-to-all-start = ((bf16[16,1,256,128]{3,2,1,0:T(8,128)(2,1)}), bf16[16,1,256,128]{3,2,1,0:T(8,128)(2,1)S(1)}, u32[]{:S(2)}, u32[]{:S(2)}) async-start(bf16[16,1,256,128]{3,2,1,0:T(8,128)(2,1)} %stack.36), calls=%async_computation | async-start | bytes 2097152 | tf_op jit(solution)/shard_map/all_to_all | solution.py:117
Sparse Core Ops, SparseCore 0:
  28.9 84.3 all-gather.9
